TPU v7x, 128 devices: a whole 4x4x4 slice. The times are simulated.
128 devices in a mesh: row: 8 (over z_hi, y), col: 16 (over x, z_lo, core).
Axes of the slice: x: 4, y: 4, z: 4 (z_hi: 2, z_lo: 2; z = z_hi * 2 + z_lo), core: 2. Of those that a mesh axis runs over, the one named last changes fastest.
Arguments:
- features: bfloat16 [16, 8192, 128], P('col', 'row'), may hold values from 0.099609375 to 3
- relu_mask: int32 [16, 8192, 128], P('col', 'row'), may hold values 0 or 1
- tiles: bfloat16 [8, 16, 184, 256, 256], P('row', 'col'), may hold values from -0.25 to 0.25
- tile_rows: int32 [8, 16, 184], P('row', 'col'), may hold values from 0 to 63, as said below
- tile_cols: int32 [8, 16, 184], P('row', 'col'), may hold values from 0 to 31
- tile_count: int32 [8, 16], P('row', 'col'), may hold values from 23 to 184, as said below
- weight: bfloat16 [128, 128], replicated, may hold values from -0.5 to 0.5
- cotangent: bfloat16 [8, 16384, 128], P('row', 'col'), may hold values from -6 to 6
Outputs:
- out_pre: bfloat16 [8, 16384, 128], P('row', 'col')
- weight_grad: float32 [128, 128], replicated
- input_grad: bfloat16 [16, 8192, 128], P('col', 'row')
Inputs may be any that keep to these rules, and one draw needn't show every extreme that they name: `tile_rows`: within one panel pair the live and dead slots name distinct (block row, block column) pairs. `tile_count`: counts differ widely between panel pairs.
All inputs are finite; a program needn't handle non-finite values. No bound on the sum of `relu_mask` on one device may be relied on, other than what follows from the above.
Results may differ from a plain program's by a relative error of at most 0.022.
Values may be sent and summed in bfloat16 or wider, within the bound.
A program may use at most 192 MiB of HBM per device.

v0:
```python
import jax
import jax.numpy as jnp
from jax import lax
from jax.sharding import PartitionSpec as P


def slot_products(tile_vals, row_ids, col_ids, source, backward):
    tile_size = tile_vals.shape[1]
    feature_width = source.shape[1]
    if backward:
        blocks = source.reshape(-1, tile_size, feature_width)[row_ids]
        products = jnp.einsum("sij,sif->sjf", tile_vals, blocks, preferred_element_type=jnp.float32)
        target_ids = col_ids
    else:
        blocks = source.reshape(-1, tile_size, feature_width)[col_ids]
        products = jnp.einsum("sij,sjf->sif", tile_vals, blocks, preferred_element_type=jnp.float32)
        target_ids = row_ids
    return (products, target_ids)


def apply_tiles(tile_vals, row_ids, col_ids, live_count, source, backward, segments):
    feature_width = source.shape[1]
    slots = tile_vals.shape[0]
    products, target_ids = slot_products(tile_vals, row_ids, col_ids, source, backward)
    live_slots = jnp.arange(slots, dtype=jnp.int32) < live_count
    targets = jnp.arange(segments, dtype=jnp.int32)[:, None] == target_ids[None, :]
    selector = jnp.where(targets & live_slots[None, :], 1.0, 0.0).astype(jnp.float32)
    total = jnp.einsum(
        "rs,sif->rif",
        selector,
        products,
        precision=lax.Precision.HIGHEST,
        preferred_element_type=jnp.float32,
    )
    return total.reshape(-1, feature_width)


def body(features, relu_mask, tiles, tile_rows, tile_cols, tile_count, weight, cotangent):
    tile_size = tiles.shape[3]
    mask_rows = relu_mask[0]
    hidden = features[0] * mask_rows.astype(jnp.bfloat16)
    tile_vals = tiles[0, 0]
    row_ids = tile_rows[0, 0]
    col_ids = tile_cols[0, 0]
    live_count = tile_count[0, 0]
    own_rows = hidden.shape[0]
    row_blocks = own_rows * lax.axis_size("col") // tile_size
    col_blocks = own_rows * lax.axis_size("row") // tile_size
    feat_panel = lax.all_gather(hidden, "row", axis=0, tiled=True)
    forward_terms = apply_tiles(
        tile_vals, row_ids, col_ids, live_count, feat_panel, False, row_blocks
    )
    forward_terms = lax.optimization_barrier(forward_terms.astype(jnp.bfloat16)).astype(jnp.float32)
    aggregate = lax.psum_scatter(
        forward_terms.astype(jnp.bfloat16), "col", scatter_dimension=0, tiled=True
    )
    out_pre = jnp.dot(aggregate, weight, preferred_element_type=jnp.float32).astype(jnp.bfloat16)
    cot_rows = cotangent[0]
    weight_term = lax.dot_general(
        aggregate, cot_rows, (((0,), (0,)), ((), ())), preferred_element_type=jnp.float32
    )
    grad_scale = 1.0 / jnp.sqrt(jnp.float32(own_rows * lax.axis_size("row") * lax.axis_size("col")))
    weight_grad = lax.psum(weight_term, ("row", "col")) * grad_scale
    grad_rows = lax.dot_general(
        cot_rows, weight, (((1,), (1,)), ((), ())), preferred_element_type=jnp.float32
    )
    grad_rows = lax.all_gather(grad_rows.astype(jnp.bfloat16), "col", axis=0, tiled=True)
    back_terms = apply_tiles(tile_vals, row_ids, col_ids, live_count, grad_rows, True, col_blocks)
    back_terms = lax.optimization_barrier(back_terms.astype(jnp.bfloat16)).astype(jnp.float32)
    summed = lax.psum_scatter(
        back_terms.astype(jnp.bfloat16), "row", scatter_dimension=0, tiled=True
    ).astype(jnp.float32)
    input_grad = (summed * mask_rows.astype(jnp.float32)).astype(jnp.bfloat16)
    return (out_pre[None], weight_grad, input_grad[None])


def solution(mesh):
    placed = (
        P("col", "row", None),
        P("col", "row", None),
        P("row", "col", None, None, None),
        P("row", "col", None),
        P("row", "col", None),
        P("row", "col"),
        P(),
        P("row", "col", None),
    )
    return jax.shard_map(
        body,
        mesh=mesh,
        in_specs=placed,
        out_specs=(P("row", "col", None), P(), P("col", "row", None)),
        check_vma=False,
    )
```

profile of v0, /device:TPU:1, one launch (start us, length us, event | category | flops | bytes accessed | tf_op | source)
XLA Modules:
  0.0 451.2 jit_solution(6644754055595961643)
XLA Ops:
  7.2 0.0 copy-start
  7.2 0.0 all-gather.6.cloned.1.call-start
  7.2 1.9 convert_multiply_fusion
  9.1 0.0 all-gather.6.cloned.1.call-update
  9.1 0.0 all-gather.4.cloned.1.call-start
  9.2 0.0 copy-done
  9.2 1.7 convolution_convert_fusion
  10.9 0.0 all-gather.4.cloned.1.call-update
  10.9 0.0 reduce-scatter.3.cloned.1.call-start
  11.6 0.7 compare_select_fusion.1
  12.3 55.5 %all-gather.6.cloned.1.call-done = bf16[1,8192,128]{2,1,0:T(8,128)(2,1)} async-done(((bf16[1,1024,128]{2,1,0:T(8,128)(2,1)}), bf16[1,8192,128]{2,1,0:T(8,128)(2,1)}) %all-gather.6.cloned.1.call-update) | async-done | bytes 2097168 | tf_op jit(solution)/shard_map/all_gather | solution.py:49
  67.9 9.7 %gather_fusion = bf16[184,256,128]{2,1,0:T(8,128)(2,1)} fusion(bf16[32,256,128]{2,1,0:T(8,128)(2,1)} %bitcast.56, s32[1024]{0:T(1024)S(1)} %pad_clamp_fusion.1), kind=kCustom, calls=%fused_computation | custom fusion | bytes 24117984 | tf_op jit(solution)/shard_map/gather | solution.py:15
  77.5 21.6 %fusion.6 = f32[184,128,256]{2,1,0:T(8,128)} fusion(bf16[184,256,128]{2,1,0:T(8,128)(2,1)} %gather_fusion, bf16[1,1,184,256,256]{4,3,2,1,0:T(8,128)(2,1)} %param.10), kind=kOutput, calls=%fused_computation.8 | convolution fusion | flops 3087007744 | bytes 60293120 | tf_op jit(solution)/shard_map/sij,sjf->sif/dot_general | solution.py:16
  99.1 0.0 copy-start.3
  99.1 24.6 %copy.13 = f32[184,128,256]{1,0,2:T(8,128)} copy(f32[184,128,256]{2,1,0:T(8,128)} %fusion.6) | data formatting | bytes 48234496 | tf_op jit(solution)/shard_map/sij,sjf->sif/dot_general | solution.py:16
  123.7 0.0 copy-done.3
  123.7 20.8 %fusion.8 = bf16[64,256,128]{2,0,1:T(8,128)(2,1)S(1)} fusion(f32[184,128,256]{1,0,2:T(8,128)} %copy.13, s32[184]{0:T(256)S(1)} %bitcast.60, pred[184]{0:T(512)(128)(4,1)S(1)} %iota_compare_fusion.2), kind=kOutput, calls=%fused_computation.10 | convolution fusion | flops 4632644096 | bytes 28312472 | tf_op jit(solution)/shard_map/rs,sif->rif/dot_general | solution.py:28
  144.5 4.7 %copy.11 = bf16[64,256,128]{2,1,0:T(8,128)(2,1)} copy(bf16[64,256,128]{2,0,1:T(8,128)(2,1)S(1)} %fusion.8) | data formatting | bytes 8388608 | tf_op jit(solution)/shard_map/convert_element_type | solution.py:53
  149.1 0.0 reduce-scatter.3.cloned.1.call-update
  149.2 0.0 reduce-scatter.5.cloned.1.call-start
  149.2 0.0 all-gather.4.cloned.1.call-done
  149.3 10.3 %gather_fusion.1 = bf16[184,256,128]{2,1,0:T(8,128)(2,1)} fusion(bf16[64,256,128]{2,1,0:T(8,128)(2,1)} %bitcast.57, s32[1024]{0:T(1024)S(1)} %pad_clamp_fusion), kind=kCustom, calls=%fused_computation.1 | custom fusion | bytes 24117984 | tf_op jit(solution)/shard_map/gather | solution.py:11
  159.5 22.0 %fusion.4 = f32[184,128,256]{2,1,0:T(8,128)} fusion(bf16[184,256,128]{2,1,0:T(8,128)(2,1)} %gather_fusion.1, bf16[1,1,184,256,256]{4,3,2,1,0:T(8,128)(2,1)} %param.10), kind=kOutput, calls=%fused_computation.6 | convolution fusion | flops 3087007744 | bytes 60293120 | tf_op jit(solution)/shard_map/sij,sif->sjf/dot_general | solution.py:12
  181.6 0.0 copy-start.4
  181.6 24.6 %copy.14 = f32[184,128,256]{1,0,2:T(8,128)} copy(f32[184,128,256]{2,1,0:T(8,128)} %fusion.4) | data formatting | bytes 48234496 | tf_op jit(solution)/shard_map/sij,sif->sjf/dot_general | solution.py:12
  206.2 0.0 copy-done.4
  206.2 0.0 copy-start.2
  206.2 0.0 copy-start.1
  206.2 17.1 %fusion.11 = bf16[32,256,128]{2,0,1:T(8,128)(2,1)S(1)} fusion(f32[184,128,256]{1,0,2:T(8,128)} %copy.14, s32[184]{0:T(256)S(1)} %bitcast.61, pred[184]{0:T(512)(128)(4,1)S(1)} %iota_compare_fusion.2), kind=kOutput, calls=%fused_computation.11 | convolution fusion | flops 2316322048 | bytes 26215320 | tf_op jit(solution)/shard_map/rs,sif->rif/dot_general | solution.py:28
  223.3 2.1 copy.12
  225.4 0.0 reduce-scatter.5.cloned.1.call-update
  225.4 0.0 all-reduce.2.cloned.1.call-start
  225.5 0.0 reduce-scatter.3.cloned.1.call-done
  225.5 1.9 fusion.18
  227.4 0.0 all-reduce.2.cloned.1.call-update
  227.4 0.0 copy-done.2
  227.4 1.9 fusion.14
  229.3 70.3 %reduce-scatter.5.cloned.1.call-done = bf16[1024,128]{1,0:T(8,128)(2,1)} async-done(((bf16[8192,128]{1,0:T(8,128)(2,1)}), bf16[1024,128]{1,0:T(8,128)(2,1)}) %reduce-scatter.5.cloned.1.call-update) | async-done | bytes 262160 | tf_op jit(solution)/shard_map/reduce_scatter | solution.py:70
  299.6 0.0 copy-done.1
  299.6 1.7 fusion.16
  301.3 141.9 %all-reduce.2.cloned.1.call-done = f32[128,128]{1,0:T(8,128)} async-done(((f32[128,128]{1,0:T(8,128)}), f32[128,128]{1,0:T(8,128)}) %all-reduce.2.cloned.1.call-update) | async-done | bytes 65552 | tf_op jit(solution)/shard_map/psum | solution.py:63
  443.2 1.5 broadcast_multiply_fusion
  (4 shorter events, 0.0 us)
Async XLA Ops:
  7.2 2.0 copy-start
  7.2 60.7 %all-gather.6.cloned.1.call-start = ((), (), s32[]{:S(2)}) async-start(), calls=%async_computation.6 | async-start | bytes 2359296 | tf_op jit(solution)/shard_map/all_gather | solution.py:49
  9.1 140.1 %all-gather.4.cloned.1.call-start = ((), (), s32[]{:S(2)}) async-start(), calls=%async_computation.4 | async-start | bytes 4456448 | tf_op jit(solution)/shard_map/all_gather | solution.py:67
  10.9 214.6 %reduce-scatter.3.cloned.1.call-start = ((), (), s32[]{:S(2)}) async-start(), calls=%async_computation.2 | async-start | bytes 4456448 | tf_op jit(solution)/shard_map/reduce_scatter | solution.py:54
  99.1 24.6 %copy-start.3 = (s32[1,1,184]{2,1,0:T(1,128)S(1)}, s32[1,1,184]{2,1,0:T(1,128)}, u32[]{:S(2)}) copy-start(s32[1,1,184]{2,1,0:T(1,128)} %param.11) | copy-start | bytes 2212
  149.2 150.4 %reduce-scatter.5.cloned.1.call-start = ((), (), s32[]{:S(2)}) async-start(), calls=%async_computation.5 | async-start | bytes 2359296 | tf_op jit(solution)/shard_map/reduce_scatter | solution.py:70
  181.6 24.6 %copy-start.4 = (s32[1,1,184]{2,1,0:T(1,128)S(1)}, s32[1,1,184]{2,1,0:T(1,128)}, u32[]{:S(2)}) copy-start(s32[1,1,184]{2,1,0:T(1,128)} %param.12) | copy-start | bytes 2212
  206.2 21.2 %copy-start.2 = (bf16[128,128]{1,0:T(8,128)(2,1)S(1)}, bf16[128,128]{1,0:T(8,128)(2,1)}, u32[]{:S(2)}) copy-start(bf16[128,128]{1,0:T(8,128)(2,1)} %param.14) | copy-start | bytes 98308
  206.2 93.4 %copy-start.1 = (s32[1,1024,128]{2,1,0:T(8,128)S(1)}, s32[1,1024,128]{2,1,0:T(8,128)}, u32[]{:S(2)}) copy-start(s32[1,1024,128]{2,1,0:T(8,128)} %param.9) | copy-start | bytes 1572868
  225.4 217.8 %all-reduce.2.cloned.1.call-start = ((), (), s32[]{:S(2)}) async-start(), calls=%async_computation.3 | async-start | bytes 131072 | tf_op jit(solution)/shard_map/psum | solution.py:63
Sparse Core Ops, SparseCore 0:
  10.9 56.9 all-gather.5
  70.1 37.8 all-gather.3
  149.3 63.9 reduce-scatter.2
  225.6 74.0 reduce-scatter.4
  305.5 137.6 all-reduce.1
where the time goes:
time: 452 us; the launch traced here: 451 us
  waiting for transfers between devices  268 us (59%)
  matrix products  86.9 us (19%)
  local copies, waits for them, and re-layouts  75.9 us (17%)
  between operations  14.5 us (3%)
  other arithmetic  5.8 us (1%)
    psum x1, waiting for transfers between devices, body(): weight_grad = lax.psum(weight_term, ('row', 'col')) * grad_scale  142 us
    reduce_scatter x1, waiting for transfers between devices, body(): lax.psum_scatter(back_terms.astype(jnp.bfloat16), 'row', scatter_dimensio...  70.3 us
    all_gather x1, waiting for transfers between devices, body(): feat_panel = lax.all_gather(hidden, 'row', axis=0, tiled=True)  55.5 us
    dot_general x2, matrix products, apply_tiles(): jnp.einsum('rs,sif->rif', selector, products, precision=lax.Precision.HIG...  37.8 us
    dot_general x1, local copies, waits for them, and re-layouts, slot_products(): jnp.einsum('sij,sif->sjf', tile_vals, blocks, preferred_element_type=jnp....  24.6 us
    dot_general x1, local copies, waits for them, and re-layouts, slot_products(): jnp.einsum('sij,sjf->sif', tile_vals, blocks, preferred_element_type=jnp....  24.6 us
    dot_general x1, matrix products, slot_products(): jnp.einsum('sij,sif->sjf', tile_vals, blocks, preferred_element_type=jnp....  22 us
    dot_general x1, matrix products, slot_products(): jnp.einsum('sij,sjf->sif', tile_vals, blocks, preferred_element_type=jnp....  21.6 us
  transfers between devices with their start and end apart: 5, of which 3 were waited for; matrix products, arithmetic and copies ran while one was open for 37% of the time, Pallas kernels for 0%

commit v1 on v0

--- a/solution.py
+++ b/solution.py
@@ -46,7 +46,10 @@
     own_rows = hidden.shape[0]
     row_blocks = own_rows * lax.axis_size("col") // tile_size
     col_blocks = own_rows * lax.axis_size("row") // tile_size
-    feat_panel = lax.all_gather(hidden, "row", axis=0, tiled=True)
+    count = lax.axis_size("row")
+    tiles_2 = jnp.stack([hidden for _ in range(count)])
+    tiles_2 = lax.all_to_all(tiles_2, "row", split_axis=0, concat_axis=0)
+    feat_panel = jnp.concatenate(tiles_2, axis=0)
     forward_terms = apply_tiles(
         tile_vals, row_ids, col_ids, live_count, feat_panel, False, row_blocks
     )

time: 452 us -> 426 us (0.942)
  waiting for transfers between devices: 268 us -> 233 us
  starting transfers between devices: 0.21 us -> 8.49 us
    all_gather x1 -> x0, waiting for transfers between devices: 55.5 us -> none  [body(): feat_panel = lax.all_gather(hidden, 'row', axis=0, tiled=True)]
    all_to_all x0 -> x1, waiting for transfers between devices: none -> 27.2 us  [body(): tiles_2 = lax.all_to_all(tiles_2, 'row', split_axis=0, concat_axis=0)]
    psum x1, waiting for transfers between devices: 142 us -> 123 us  [body(): weight_grad = lax.psum(weight_term, ('row', 'col')) * grad_scale]
    reduce_scatter x1, waiting for transfers between devices: 0.02 us -> 9.41 us  [body(): lax.psum_scatter(forward_terms.astype(jnp.bfloat16), 'col', scatter_dimen...]
    all_to_all x0 -> x1, starting transfers between devices: none -> 8.33 us  [body(): tiles_2 = lax.all_to_all(tiles_2, 'row', split_axis=0, concat_axis=0)]
  transfers between devices with their start and end apart: 5 -> 5, of which waited for: 3 -> 4; matrix products, arithmetic and copies ran while one was open for 37% -> 38% of each run, Pallas kernels for 0% -> 0%
where the time goes in v1:
time: 426 us; the launch traced here: 424 us
  waiting for transfers between devices  233 us (55%)
  matrix products  85.9 us (20%)
  local copies, waits for them, and re-layouts  76.7 us (18%)
  between operations  14.5 us (3%)
  starting transfers between devices  8.49 us (2%)
  other arithmetic  5.07 us (1%)
    psum x1, waiting for transfers between devices, body(): weight_grad = lax.psum(weight_term, ('row', 'col')) * grad_scale  123 us
    reduce_scatter x1, waiting for transfers between devices, body(): lax.psum_scatter(back_terms.astype(jnp.bfloat16), 'row', scatter_dimensio...  73.6 us
    dot_general x2, matrix products, apply_tiles(): jnp.einsum('rs,sif->rif', selector, products, precision=lax.Precision.HIG...  37.9 us
    all_to_all x1, waiting for transfers between devices, body(): tiles_2 = lax.all_to_all(tiles_2, 'row', split_axis=0, concat_axis=0)  27.2 us
    dot_general x1, local copies, waits for them, and re-layouts, slot_products(): jnp.einsum('sij,sif->sjf', tile_vals, blocks, preferred_element_type=jnp....  24.5 us
    dot_general x1, local copies, waits for them, and re-layouts, slot_products(): jnp.einsum('sij,sjf->sif', tile_vals, blocks, preferred_element_type=jnp....  24.5 us
    dot_general x1, matrix products, slot_products(): jnp.einsum('sij,sif->sjf', tile_vals, blocks, preferred_element_type=jnp....  22.3 us
    dot_general x1, matrix products, slot_products(): jnp.einsum('sij,sjf->sif', tile_vals, blocks, preferred_element_type=jnp....  21.2 us
  transfers between devices with their start and end apart: 5, of which 4 were waited for; matrix products, arithmetic and copies ran while one was open for 38% of the time, Pallas kernels for 0%

profile of v1, /device:TPU:1, one launch (start us, length us, event | category | flops | bytes accessed | tf_op | source)
XLA Modules:
  0.0 424.1 jit_solution(17459217903747370980)
XLA Ops:
  7.2 0.0 copy-start
  7.2 0.0 all-gather.2.cloned.1.call-start
  7.2 0.9 copy-done
  8.1 1.7 convolution_convert_fusion
  9.8 0.0 all-gather.2.cloned.1.call-update
  9.8 1.2 multiply_bitcast_fusion
  11.0 1.6 stack.5
  12.6 8.3 %all-to-all-start = ((bf16[8,1024,128]{2,1,0:T(8,128)(2,1)}), bf16[8,1024,128]{2,1,0:T(8,128)(2,1)S(1)}, u32[]{:S(2)}, u32[]{:S(2)}) async-start(bf16[8,1024,128]{2,1,0:T(8,128)(2,1)} %stack.5), calls=%async_computation | async-start | bytes 4194304 | tf_op jit(solution)/shard_map/all_to_all | solution.py:51
  20.9 0.0 reduce-scatter.3.cloned.1.call-start
  21.6 0.7 compare_select_fusion.1
  22.3 27.2 %all-to-all-done = bf16[8,1024,128]{2,1,0:T(8,128)(2,1)S(1)} async-done(((bf16[8,1024,128]{2,1,0:T(8,128)(2,1)}), bf16[8,1024,128]{2,1,0:T(8,128)(2,1)S(1)}, u32[]{:S(2)}, u32[]{:S(2)}) %all-to-all-start) | async-done | bytes 2097184 | tf_op jit(solution)/shard_map/all_to_all | solution.py:51
  49.5 8.1 %gather_fusion = bf16[184,256,128]{2,1,0:T(8,128)(2,1)} fusion(bf16[32,256,128]{2,1,0:T(8,128)(2,1)S(1)} %bitcast.58, s32[1024]{0:T(1024)S(1)} %pad_clamp_fusion.1), kind=kCustom, calls=%fused_computation | custom fusion | bytes 24117984 | tf_op jit(solution)/shard_map/gather | solution.py:15
  57.6 21.2 %fusion.6 = f32[184,128,256]{2,1,0:T(8,128)} fusion(bf16[184,256,128]{2,1,0:T(8,128)(2,1)} %gather_fusion, bf16[1,1,184,256,256]{4,3,2,1,0:T(8,128)(2,1)} %param.10), kind=kOutput, calls=%fused_computation.8 | convolution fusion | flops 3087007744 | bytes 60293120 | tf_op jit(solution)/shard_map/sij,sjf->sif/dot_general | solution.py:16
  78.8 0.0 copy-start.4
  78.8 24.5 %copy.13 = f32[184,128,256]{1,0,2:T(8,128)} copy(f32[184,128,256]{2,1,0:T(8,128)} %fusion.6) | data formatting | bytes 48234496 | tf_op jit(solution)/shard_map/sij,sjf->sif/dot_general | solution.py:16
  103.4 0.0 copy-done.4
  103.4 20.8 %fusion.8 = bf16[64,256,128]{2,0,1:T(8,128)(2,1)S(1)} fusion(f32[184,128,256]{1,0,2:T(8,128)} %copy.13, s32[184]{0:T(256)S(1)} %bitcast.62, pred[184]{0:T(512)(128)(4,1)S(1)} %iota_compare_fusion.2), kind=kOutput, calls=%fused_computation.10 | convolution fusion | flops 4632644096 | bytes 28312472 | tf_op jit(solution)/shard_map/rs,sif->rif/dot_general | solution.py:28
  124.2 4.7 %copy.11 = bf16[64,256,128]{2,1,0:T(8,128)(2,1)} copy(bf16[64,256,128]{2,0,1:T(8,128)(2,1)S(1)} %fusion.8) | data formatting | bytes 8388608 | tf_op jit(solution)/shard_map/convert_element_type | solution.py:56
  128.8 0.0 reduce-scatter.3.cloned.1.call-update
  128.8 0.0 all-reduce.2.cloned.1.call-start
  128.9 0.0 all-gather.2.cloned.1.call-done
  128.9 10.3 %gather_fusion.1 = bf16[184,256,128]{2,1,0:T(8,128)(2,1)} fusion(bf16[64,256,128]{2,1,0:T(8,128)(2,1)} %bitcast.59, s32[1024]{0:T(1024)S(1)} %pad_clamp_fusion), kind=kCustom, calls=%fused_computation.1 | custom fusion | bytes 24117984 | tf_op jit(solution)/shard_map/gather | solution.py:11
  139.2 22.3 %fusion.4 = f32[184,128,256]{2,1,0:T(8,128)} fusion(bf16[184,256,128]{2,1,0:T(8,128)(2,1)} %gather_fusion.1, bf16[1,1,184,256,256]{4,3,2,1,0:T(8,128)(2,1)} %param.10), kind=kOutput, calls=%fused_computation.6 | convolution fusion | flops 3087007744 | bytes 60293120 | tf_op jit(solution)/shard_map/sij,sif->sjf/dot_general | solution.py:12
  161.5 0.0 copy-start.5
  161.5 24.5 %copy.14 = f32[184,128,256]{1,0,2:T(8,128)} copy(f32[184,128,256]{2,1,0:T(8,128)} %fusion.4) | data formatting | bytes 48234496 | tf_op jit(solution)/shard_map/sij,sif->sjf/dot_general | solution.py:12
  186.0 9.4 %reduce-scatter.3.cloned.1.call-done = bf16[1024,128]{1,0:T(8,128)(2,1)} async-done(((bf16[16384,128]{1,0:T(8,128)(2,1)}), bf16[1024,128]{1,0:T(8,128)(2,1)}) %reduce-scatter.3.cloned.1.call-update) | async-done | bytes 262160 | tf_op jit(solution)/shard_map/reduce_scatter | solution.py:57
  195.5 1.8 fusion.18
  197.3 0.0 all-reduce.2.cloned.1.call-update
  197.3 0.0 reduce-scatter.5.cloned.1.call-start
  197.4 0.0 copy-done.5
  197.4 0.0 copy-start.2
  197.4 0.0 copy-start.3
  197.4 0.0 copy-start.1
  197.4 17.1 %fusion.11 = bf16[32,256,128]{2,0,1:T(8,128)(2,1)S(1)} fusion(f32[184,128,256]{1,0,2:T(8,128)} %copy.14, s32[184]{0:T(256)S(1)} %bitcast.63, pred[184]{0:T(512)(128)(4,1)S(1)} %iota_compare_fusion.2), kind=kOutput, calls=%fused_computation.11 | convolution fusion | flops 2316322048 | bytes 26215320 | tf_op jit(solution)/shard_map/rs,sif->rif/dot_general | solution.py:28
  214.5 2.1 copy.12
  216.6 0.0 reduce-scatter.5.cloned.1.call-update
  216.7 0.0 copy-done.2
  216.7 0.0 copy-done.3
  216.7 0.9 fusion.14
  217.6 123.2 %all-reduce.2.cloned.1.call-done = f32[128,128]{1,0:T(8,128)} async-done(((f32[128,128]{1,0:T(8,128)}), f32[128,128]{1,0:T(8,128)}) %all-reduce.2.cloned.1.call-update) | async-done | bytes 65552 | tf_op jit(solution)/shard_map/psum | solution.py:66
  340.8 1.5 broadcast_multiply_fusion
  342.2 73.6 %reduce-scatter.5.cloned.1.call-done = bf16[1024,128]{1,0:T(8,128)(2,1)} async-done(((bf16[8192,128]{1,0:T(8,128)(2,1)}), bf16[1024,128]{1,0:T(8,128)(2,1)}) %reduce-scatter.5.cloned.1.call-update) | async-done | bytes 262160 | tf_op jit(solution)/shard_map/reduce_scatter | solution.py:73
  415.8 0.0 copy-done.1
  415.8 1.7 fusion.16
  (4 shorter events, 0.0 us)
Async XLA Ops:
  7.2 1.0 copy-start
  7.2 121.8 %all-gather.2.cloned.1.call-start = ((), (), s32[]{:S(2)}) async-start(), calls=%async_computation.5 | async-start | bytes 4456448 | tf_op jit(solution)/shard_map/all_gather | solution.py:70
  12.6 36.9 %all-to-all-start = ((bf16[8,1024,128]{2,1,0:T(8,128)(2,1)}), bf16[8,1024,128]{2,1,0:T(8,128)(2,1)S(1)}, u32[]{:S(2)}, u32[]{:S(2)}) async-start(bf16[8,1024,128]{2,1,0:T(8,128)(2,1)} %stack.5), calls=%async_computation | async-start | bytes 4194304 | tf_op jit(solution)/shard_map/all_to_all | solution.py:51
  20.9 174.5 %reduce-scatter.3.cloned.1.call-start = ((), (), s32[]{:S(2)}) async-start(), calls=%async_computation.3 | async-start | bytes 4456448 | tf_op jit(solution)/shard_map/reduce_scatter | solution.py:57
  78.8 24.5 %copy-start.4 = (s32[1,1,184]{2,1,0:T(1,128)S(1)}, s32[1,1,184]{2,1,0:T(1,128)}, u32[]{:S(2)}) copy-start(s32[1,1,184]{2,1,0:T(1,128)} %param.11) | copy-start | bytes 2212
  128.8 211.9 %all-reduce.2.cloned.1.call-start = ((), (), s32[]{:S(2)}) async-start(), calls=%async_computation.4 | async-start | bytes 131072 | tf_op jit(solution)/shard_map/psum | solution.py:66
  161.5 35.9 %copy-start.5 = (s32[1,1,184]{2,1,0:T(1,128)S(1)}, s32[1,1,184]{2,1,0:T(1,128)}, u32[]{:S(2)}) copy-start(s32[1,1,184]{2,1,0:T(1,128)} %param.12) | copy-start | bytes 2212
  197.3 218.5 %reduce-scatter.5.cloned.1.call-start = ((), (), s32[]{:S(2)}) async-start(), calls=%async_computation.6 | async-start | bytes 2359296 | tf_op jit(solution)/shard_map/reduce_scatter | solution.py:73
  197.4 19.3 %copy-start.2 = (bf16[1024,128]{1,0:T(8,128)(2,1)S(1)}, bf16[1024,128]{1,0:T(8,128)(2,1)}, u32[]{:S(2)}) copy-start(bf16[1024,128]{1,0:T(8,128)(2,1)} %reduce-scatter.3.cloned.1.call-done) | copy-start | bytes 786436
  197.4 19.3 %copy-start.3 = (bf16[128,128]{1,0:T(8,128)(2,1)S(1)}, bf16[128,128]{1,0:T(8,128)(2,1)}, u32[]{:S(2)}) copy-start(bf16[128,128]{1,0:T(8,128)(2,1)} %param.14) | copy-start | bytes 98308
  197.4 218.4 %copy-start.1 = (s32[1,1024,128]{2,1,0:T(8,128)S(1)}, s32[1,1024,128]{2,1,0:T(8,128)}, u32[]{:S(2)}) copy-start(s32[1,1024,128]{2,1,0:T(8,128)} %param.9) | copy-start | bytes 1572868
Sparse Core Ops, SparseCore 0:
  10.3 60.7 all-gather.1
  129.0 66.4 reduce-scatter.2
  200.8 139.9 all-reduce.1
  344.8 70.9 reduce-scatter.4
